TPU v7x, 32 devices: a whole 2x2x4 slice. The times are simulated.
32 devices in a mesh: dp: 8 (over z, y), tensor: 4 (over x, core).
Axes of the slice: x: 2, y: 2, z: 4, core: 2. Of those that a mesh axis runs over, the one named last changes fastest.
Arguments:
- block_input: bfloat16 [8192, 1536], P(('dp', 'tensor')), may hold values from -6 to 6
- segment_ids: int32 [8, 1024], P('dp'), may hold values from 0 to 3, as said below
- gain_attn: float32 [1536], replicated, may hold values from 0.5 to 1.5
- w_query: bfloat16 [1536, 1536], P('dp', 'tensor'), may hold values from -0.15625 to 0.15625
- b_query: float32 [1536], P('tensor'), may hold values from -3 to 3
- w_keyval: bfloat16 [1536, 512], P('dp'), may hold values from -0.15625 to 0.15625
- b_keyval: float32 [512], replicated, may hold values from -3 to 3
- w_out: bfloat16 [1536, 1536], P('tensor', 'dp'), may hold values from -0.625 to 0.625
- gain_ffn: float32 [1536], replicated, may hold values from 0.5 to 1.5
- w_gate: bfloat16 [1536, 8960], P('dp', 'tensor'), may hold values from -0.15625 to 0.15625
- w_up: bfloat16 [1536, 8960], P('dp', 'tensor'), may hold values from -0.15625 to 0.15625
- w_down: bfloat16 [8960, 1536], P('tensor', 'dp'), may hold values from -0.0625 to 0.0625
- cotangent: bfloat16 [8192, 1536], P(('dp', 'tensor')), may hold values from -6 to 6
Outputs:
- block_output: bfloat16 [8192, 1536], P(('dp', 'tensor'))
- grad_input: bfloat16 [8192, 1536], P(('dp', 'tensor'))
- grad_gain_attn: float32 [1536], P(('dp', 'tensor'))
- grad_w_query: float32 [1536, 1536], P('dp', 'tensor')
- grad_b_query: float32 [1536], P(('dp', 'tensor'))
- grad_w_keyval: float32 [1536, 512], P(('dp', 'tensor'))
- grad_b_keyval: float32 [512], P(('dp', 'tensor'))
- grad_w_out: float32 [1536, 1536], P('tensor', 'dp')
- grad_gain_ffn: float32 [1536], P(('dp', 'tensor'))
- grad_w_gate: float32 [1536, 8960], P('dp', 'tensor')
- grad_w_up: float32 [1536, 8960], P('dp', 'tensor')
- grad_w_down: float32 [8960, 1536], P('tensor', 'dp')
Inputs may be any that keep to these rules, and one draw needn't show every extreme that they name: `segment_ids`: ids start at 0 and never fall along a sequence, each rising by one at a document's start; a sequence holds 2 to 4 documents, each of 204 tokens or more; some sequence holds 4.
All inputs are finite; a program needn't handle non-finite values.
Results may differ from a plain program's by a relative error of at most 0.018.
Values may be sent and summed in bfloat16 or wider, within the bound.
No kernel may reach another device: no remote copies, remote signals or barrier semaphores. Data moves between devices by JAX's collectives and lax.ppermute only.
A program may use at most 256 MiB of HBM per device.

v0:
```python
import math
import jax
import jax.numpy as jnp
from jax import lax
from jax.sharding import PartitionSpec as P

HQ = 12
KV = 2
HD = 128
epsilon = 1e-06
rope_base = 1000000.0
masked_score = -1e30


def matmul(left, right):
    return jnp.dot(left, right, preferred_element_type=jnp.float32)


def positions_of(segment_row):
    index_row = jnp.arange(segment_row.shape[0], dtype=jnp.int32)
    starts = jnp.concatenate(
        [jnp.ones((1,), jnp.int32), (segment_row[1:] != segment_row[:-1]).astype(jnp.int32)]
    )
    first_index = lax.cummax(jnp.where(starts > 0, index_row, 0), axis=0)
    return index_row - first_index


def allowed_of(segment_row):
    index_row = jnp.arange(segment_row.shape[0], dtype=jnp.int32)
    causal = index_row[:, None] >= index_row[None, :]
    return causal & (segment_row[:, None] == segment_row[None, :])


def rotary(positions):
    inverse = rope_base ** (-(jnp.arange(HD // 2, dtype=jnp.float32) * 2.0 / HD))
    angles = positions.astype(jnp.float32)[:, None] * inverse[None, :]
    angles = jnp.concatenate([angles, angles], axis=1)
    return (jnp.cos(angles), jnp.sin(angles))


def turn(values_in, cosine_table, sine_table):
    half_size = values_in.shape[-1] // 2
    rolled = jnp.concatenate([-values_in[..., half_size:], values_in[..., :half_size]], axis=-1)
    return values_in * cosine_table + rolled * sine_table


def norm_forward(values_in):
    row_scale = lax.rsqrt(jnp.mean(values_in * values_in, axis=-1, keepdims=True) + epsilon)
    return (values_in * row_scale, row_scale)


def norm_backward(grad_out, normed, row_scale, gain_vec):
    grad_normed = grad_out * gain_vec
    grad_in = row_scale * (
        grad_normed - normed * jnp.mean(grad_normed * normed, axis=-1, keepdims=True)
    )
    return (grad_in, jnp.sum(grad_out * normed, axis=0))


def gather_three(first, second, third):
    return (
        lax.all_gather(first, "dp", axis=0, tiled=True),
        lax.all_gather(second, "dp", axis=0, tiled=True),
        lax.all_gather(third, "dp", axis=1, tiled=True),
    )


def masked_scores(query_rot, key_rot, segment_row):
    raw_scores = jnp.einsum(
        "qhd,kd->hqk", query_rot, key_rot, preferred_element_type=jnp.float32
    ) / math.sqrt(HD)
    return jnp.where(allowed_of(segment_row)[None], raw_scores, masked_score)


def attend(query_rot, key_rot, value_rows, segment_row):
    scores = masked_scores(query_rot, key_rot, segment_row)
    row_max = jnp.max(scores, axis=2, keepdims=True)
    log_total = row_max + jnp.log(jnp.sum(jnp.exp(scores - row_max), axis=2, keepdims=True))
    probs_low = jnp.exp(scores - log_total).astype(jnp.bfloat16)
    attn_result = jnp.einsum(
        "hqk,kd->qhd", probs_low, value_rows, preferred_element_type=jnp.float32
    )
    return (attn_result, log_total)


def attend_back(query_rot, key_rot, value_rows, segment_row, log_total, attn_result, grad_context):
    scores = masked_scores(query_rot, key_rot, segment_row)
    attn_probs = jnp.exp(scores - log_total)
    probs_low = attn_probs.astype(jnp.bfloat16)
    grad_probs = jnp.einsum(
        "qhd,kd->hqk", grad_context, value_rows, preferred_element_type=jnp.float32
    )
    row_delta = jnp.sum(grad_context.astype(jnp.float32) * attn_result, axis=2).T[:, :, None]
    grad_scores = (attn_probs * (grad_probs - row_delta)).astype(jnp.bfloat16)
    grad_query_rot = jnp.einsum(
        "hqk,kd->qhd", grad_scores, key_rot, preferred_element_type=jnp.float32
    ) / math.sqrt(HD)
    grad_key_rot = jnp.einsum(
        "hqk,qhd->kd", grad_scores, query_rot, preferred_element_type=jnp.float32
    ) / math.sqrt(HD)
    grad_value = jnp.einsum(
        "hqk,qhd->kd", probs_low, grad_context, preferred_element_type=jnp.float32
    )
    return (grad_query_rot, grad_key_rot, grad_value)


def local(
    block_input,
    segment_ids,
    gain_attn,
    w_query,
    b_query,
    w_keyval,
    b_keyval,
    w_out,
    gain_ffn,
    w_gate,
    w_up,
    w_down,
    cotangent,
):
    tensor_index = lax.axis_index("tensor")
    seq_count = segment_ids.shape[0]
    seq_length = segment_ids.shape[1]
    row_count = seq_count * seq_length
    local_heads = b_query.shape[0] // HD
    head_kv = tensor_index * local_heads // (HQ // KV)
    rows_float = block_input.astype(jnp.float32)
    normed_one, scale_one = norm_forward(rows_float)
    act_one = lax.all_gather(
        (normed_one * gain_attn).astype(jnp.bfloat16), "tensor", axis=0, tiled=True
    )
    query_w, keyval_w, out_w = gather_three(w_query, w_keyval, w_out)
    query_rows = matmul(act_one, query_w) + b_query
    keyval = matmul(act_one, keyval_w) + b_keyval
    key_rows = lax.dynamic_slice_in_dim(keyval, head_kv * HD, HD, 1)
    value_rows = lax.dynamic_slice_in_dim(keyval, KV * HD + head_kv * HD, HD, 1).astype(
        jnp.bfloat16
    )
    positions = jax.vmap(positions_of)(segment_ids).reshape(row_count)
    cosine_table, sine_table = rotary(positions)
    cos_heads = cosine_table[:, None, :]
    sin_heads = sine_table[:, None, :]
    query_rot = turn(query_rows.reshape(row_count, local_heads, HD), cos_heads, sin_heads).astype(
        jnp.bfloat16
    )
    key_rot = turn(key_rows, cosine_table, sine_table).astype(jnp.bfloat16)
    query_seq = query_rot.reshape(seq_count, seq_length, local_heads, HD)
    key_seq = key_rot.reshape(seq_count, seq_length, HD)
    value_seq = value_rows.reshape(seq_count, seq_length, HD)
    attn_result, log_total = lax.map(
        lambda seq_items: attend(*seq_items), (query_seq, key_seq, value_seq, segment_ids)
    )
    context = attn_result.astype(jnp.bfloat16).reshape(row_count, local_heads * HD)
    hidden = rows_float + lax.psum_scatter(
        matmul(context, out_w), "tensor", scatter_dimension=0, tiled=True
    )
    normed_two, scale_two = norm_forward(hidden)
    act_two = lax.all_gather(
        (normed_two * gain_ffn).astype(jnp.bfloat16), "tensor", axis=0, tiled=True
    )
    gate_w, up_w, down_w = gather_three(w_gate, w_up, w_down)
    gate_pre = matmul(act_two, gate_w)
    up_part = matmul(act_two, up_w)
    sigmoid_gate = jax.nn.sigmoid(gate_pre)
    silu_gate = gate_pre * sigmoid_gate
    mixed_rows = (silu_gate * up_part).astype(jnp.bfloat16)
    block_out = (
        hidden
        + lax.psum_scatter(
            matmul(mixed_rows, down_w).astype(jnp.bfloat16),
            "tensor",
            scatter_dimension=0,
            tiled=True,
        ).astype(jnp.float32)
    ).astype(jnp.bfloat16)
    cot_rows = lax.all_gather(cotangent, "tensor", axis=0, tiled=True)
    grad_mixed = matmul(cot_rows, down_w.T)
    grad_gate = (
        grad_mixed * up_part * sigmoid_gate * (1.0 + gate_pre * (1.0 - sigmoid_gate))
    ).astype(jnp.bfloat16)
    grad_up = (grad_mixed * silu_gate).astype(jnp.bfloat16)
    grad_gate_w = matmul(act_two.T, grad_gate)
    grad_up_w = matmul(act_two.T, grad_up)
    grad_down_w = matmul(mixed_rows.T, cot_rows)
    grad_act_two = lax.psum_scatter(
        matmul(grad_gate, gate_w.T) + matmul(grad_up, up_w.T),
        "tensor",
        scatter_dimension=0,
        tiled=True,
    )
    back_two, gain_two = norm_backward(grad_act_two, normed_two, scale_two, gain_ffn)
    grad_hidden = cotangent.astype(jnp.float32) + back_two
    grad_attn = lax.all_gather(grad_hidden.astype(jnp.bfloat16), "tensor", axis=0, tiled=True)
    grad_out_w = matmul(context.T, grad_attn)
    grad_context = (
        matmul(grad_attn, out_w.T)
        .astype(jnp.bfloat16)
        .reshape(seq_count, seq_length, local_heads, HD)
    )
    grad_query_rot, grad_key_rot, grad_value = lax.map(
        lambda seq_items: attend_back(*seq_items),
        (query_seq, key_seq, value_seq, segment_ids, log_total, attn_result, grad_context),
    )
    grad_query = turn(
        grad_query_rot.reshape(row_count, local_heads, HD), cos_heads, -sin_heads
    ).reshape(row_count, local_heads * HD)
    grad_key = turn(grad_key_rot.reshape(row_count, HD), cosine_table, -sine_table)
    grad_value = grad_value.reshape(row_count, HD)
    grad_query_low = grad_query.astype(jnp.bfloat16)
    kv_columns = jnp.zeros((row_count, keyval.shape[1]), jnp.bfloat16)
    kv_columns = lax.dynamic_update_slice_in_dim(
        kv_columns, grad_key.astype(jnp.bfloat16), head_kv * HD, 1
    )
    kv_columns = lax.dynamic_update_slice_in_dim(
        kv_columns, grad_value.astype(jnp.bfloat16), KV * HD + head_kv * HD, 1
    )
    bias_keyval = jnp.zeros((keyval.shape[1],), jnp.float32)
    bias_keyval = lax.dynamic_update_slice_in_dim(
        bias_keyval, jnp.sum(grad_key, axis=0), head_kv * HD, 0
    )
    bias_keyval = lax.dynamic_update_slice_in_dim(
        bias_keyval, jnp.sum(grad_value, axis=0), KV * HD + head_kv * HD, 0
    )
    bias_query = lax.dynamic_update_slice_in_dim(
        jnp.zeros((HQ * HD,), jnp.float32),
        jnp.sum(grad_query, axis=0),
        tensor_index * local_heads * HD,
        0,
    )
    grad_query_w = matmul(act_one.T, grad_query_low)
    grad_keyval_w = matmul(act_one.T, kv_columns)
    grad_act_one = lax.psum_scatter(
        (matmul(grad_query_low, query_w.T) + matmul(kv_columns, keyval_w.T)).astype(jnp.bfloat16),
        "tensor",
        scatter_dimension=0,
        tiled=True,
    ).astype(jnp.float32)
    back_one, gain_one = norm_backward(grad_act_one, normed_one, scale_one, gain_attn)
    grad_rows = (grad_hidden + back_one).astype(jnp.bfloat16)
    keyval_share, gain_one_share, gain_two_share, query_bias_share, keyval_bias_share = (
        lax.psum_scatter(grad_keyval_w, ("dp", "tensor"), scatter_dimension=0, tiled=True),
        lax.psum_scatter(gain_one, ("dp", "tensor"), scatter_dimension=0, tiled=True),
        lax.psum_scatter(gain_two, ("dp", "tensor"), scatter_dimension=0, tiled=True),
        lax.psum_scatter(bias_query, ("dp", "tensor"), scatter_dimension=0, tiled=True),
        lax.psum_scatter(bias_keyval, ("dp", "tensor"), scatter_dimension=0, tiled=True),
    )
    query_share, out_share, gate_share, up_share, down_share = (
        lax.psum_scatter(
            grad_query_w.astype(jnp.bfloat16), "dp", scatter_dimension=0, tiled=True
        ).astype(jnp.float32),
        lax.psum_scatter(
            grad_out_w.astype(jnp.bfloat16), "dp", scatter_dimension=1, tiled=True
        ).astype(jnp.float32),
        lax.psum_scatter(
            grad_gate_w.astype(jnp.bfloat16), "dp", scatter_dimension=0, tiled=True
        ).astype(jnp.float32),
        lax.psum_scatter(
            grad_up_w.astype(jnp.bfloat16), "dp", scatter_dimension=0, tiled=True
        ).astype(jnp.float32),
        lax.psum_scatter(
            grad_down_w.astype(jnp.bfloat16), "dp", scatter_dimension=1, tiled=True
        ).astype(jnp.float32),
    )
    return (
        block_out,
        grad_rows,
        gain_one_share,
        query_share,
        query_bias_share,
        keyval_share,
        keyval_bias_share,
        out_share,
        gain_two_share,
        gate_share,
        up_share,
        down_share,
    )


def solution(mesh):
    placed = (
        P(("dp", "tensor"), None),
        P("dp", None),
        P(),
        P("dp", "tensor"),
        P("tensor"),
        P("dp", None),
        P(),
        P("tensor", "dp"),
        P(),
        P("dp", "tensor"),
        P("dp", "tensor"),
        P("tensor", "dp"),
        P(("dp", "tensor"), None),
    )
    return jax.shard_map(
        local,
        mesh=mesh,
        in_specs=placed,
        out_specs=(
            P(("dp", "tensor"), None),
            P(("dp", "tensor"), None),
            P(("dp", "tensor")),
            P("dp", "tensor"),
            P(("dp", "tensor")),
            P(("dp", "tensor"), None),
            P(("dp", "tensor")),
            P("tensor", "dp"),
            P(("dp", "tensor")),
            P("dp", "tensor"),
            P("dp", "tensor"),
            P("tensor", "dp"),
        ),
        check_vma=False,
    )
```

profile of v0, /device:TPU:0, one launch (start us, length us, event | category | flops | bytes accessed | tf_op | source)
XLA Modules:
  0.0 1482.0 jit_solution(15097303568250098657)
XLA Ops:
  14.6 39.4 %all-gather.15.cloned.1.call-done = bf16[1536,384]{1,0:T(8,128)(2,1)} async-done(((bf16[192,384]{1,0:T(8,128)(2,1)}), bf16[1536,384]{1,0:T(8,128)(2,1)}) %all-gather.15.cloned.1.call-update) | async-done | bytes 1179664 | tf_op jit(solution)/shard_map/all_gather | solution.py:62
  54.0 29.5 %all-gather.11.cloned.1.call-done = bf16[1024,1536]{1,0:T(8,128)(2,1)} async-done(((bf16[256,1536]{1,0:T(8,128)(2,1)}), bf16[1024,1536]{1,0:T(8,128)(2,1)}) %all-gather.11.cloned.1.call-update) | async-done | bytes 3145744 | tf_op jit(solution)/shard_map/all_gather | solution.py:130
  83.5 3.6 convolution_add_fusion.2
  88.2 41.7 %all-gather.13.cloned.1.call-done = bf16[1536,512]{1,0:T(8,128)(2,1)} async-done(((bf16[192,512]{1,0:T(8,128)(2,1)}), bf16[1536,512]{1,0:T(8,128)(2,1)}) %all-gather.13.cloned.1.call-update) | async-done | bytes 1572880 | tf_op jit(solution)/shard_map/all_gather | solution.py:63
  129.9 4.2 convolution_add_fusion.1
  134.9 3.4 broadcast_multiply_fusion
  138.9 6.0 fusion.4
  144.9 7.3 exponential_reduce_fusion
  152.2 9.5 bitcast_convert_fusion
  161.7 10.1 all-gather.17.cloned.1.call-done
  171.8 5.7 fusion.46
  178.2 56.6 %reduce-scatter.11.cloned.1.call-done = f32[256,1536]{1,0:T(8,128)} async-done(((f32[1024,1536]{1,0:T(8,128)}), f32[256,1536]{1,0:T(8,128)}) %reduce-scatter.11.cloned.1.call-update) | async-done | bytes 1572880 | tf_op jit(solution)/shard_map/reduce_scatter | solution.py:155
  239.8 106.2 %all-gather.21.cloned.1.call-done = bf16[1536,2240]{1,0:T(8,128)(2,1)} async-done(((bf16[192,2240]{1,0:T(8,128)(2,1)}), bf16[1536,2240]{1,0:T(8,128)(2,1)}) %all-gather.21.cloned.1.call-update) | async-done | bytes 6881296 | tf_op jit(solution)/shard_map/all_gather | solution.py:62
  346.0 29.0 %all-gather.19.cloned.1.call-done = bf16[1024,1536]{1,0:T(8,128)(2,1)} async-done(((bf16[256,1536]{1,0:T(8,128)(2,1)}), bf16[1024,1536]{1,0:T(8,128)(2,1)}) %all-gather.19.cloned.1.call-update) | async-done | bytes 3145744 | tf_op jit(solution)/shard_map/all_gather | solution.py:159
  374.9 13.3 fusion.47
  388.3 97.9 %all-gather.23.cloned.1.call-done = bf16[1536,2240]{1,0:T(8,128)(2,1)} async-done(((bf16[192,2240]{1,0:T(8,128)(2,1)}), bf16[1536,2240]{1,0:T(8,128)(2,1)}) %all-gather.23.cloned.1.call-update) | async-done | bytes 6881296 | tf_op jit(solution)/shard_map/all_gather | solution.py:63
  486.2 13.2 fusion.48
  499.4 15.2 %all-gather.27.cloned.1.call-done = bf16[1024,1536]{1,0:T(8,128)(2,1)} async-done(((bf16[256,1536]{1,0:T(8,128)(2,1)}), bf16[1024,1536]{1,0:T(8,128)(2,1)}) %all-gather.27.cloned.1.call-update) | async-done | bytes 3145744 | tf_op jit(solution)/shard_map/all_gather | solution.py:177
  514.6 111.1 %all-gather.25.cloned.1.call-done = bf16[2240,1536]{0,1:T(8,128)(2,1)} async-done(((bf16[2240,192]{0,1:T(8,128)(2,1)}), bf16[2240,1536]{0,1:T(8,128)(2,1)}) %all-gather.25.cloned.1.call-update) | async-done | bytes 6881296 | tf_op jit(solution)/shard_map/all_gather | solution.py:64
  625.7 20.2 %multiply_convert_fusion = (bf16[1024,2240]{0,1:T(8,128)(2,1)}, bf16[1024,2240]{0,1:T(8,128)(2,1)}, bf16[1024,2240]{0,1:T(8,128)(2,1)}) fusion(f32[1024,2240]{0,1:T(8,128)} %fusion.47, f32[1024,2240]{0,1:T(8,128)} %fusion.48, bf16[1024,1536]{1,0:T(8,128)(2,1)} %all-gather.27.cloned.1.call-done, bf16[2240,1536]{0,1:T(8,128)(2,1)} %all-gather.25.cloned.1.call-done), kind=kOutput, calls=%fused_computation.10 | convolution fusion | flops 7080837120 | bytes 42139648 | tf_op jit(solution)/shard_map/dot_general | solution.py:16
  645.8 11.4 fusion.49
  657.3 10.1 convolution_add_fusion
  667.4 56.6 %reduce-scatter.15.cloned.1.call-done = f32[256,1536]{1,0:T(8,128)} async-done(((f32[1024,1536]{1,0:T(8,128)}), f32[256,1536]{1,0:T(8,128)}) %reduce-scatter.15.cloned.1.call-update) | async-done | bytes 1572880 | tf_op jit(solution)/shard_map/reduce_scatter | solution.py:186
  727.5 12.3 convolution_convert_fusion.2
  739.9 12.6 convolution_convert_fusion.1
  752.6 12.4 convolution_convert_fusion
  765.1 4.3 convolution_convert_fusion.6
  770.3 2.9 convolution_convert_fusion.4
  773.4 9.4 fusion.1
  787.9 2.9 convolution_convert_fusion.5
  791.3 9.1 fusion.45
  801.5 5.2 fusion.22
  806.8 2.3 fusion.43
  812.1 3.6 add_convert_fusion
  816.0 12.5 convolution_convert_fusion.3
  829.8 5.4 fusion.51
  835.2 53.8 %reduce-scatter.25.cloned.1.call-done = bf16[192,2240]{1,0:T(8,128)(2,1)} async-done(((bf16[1536,2240]{1,0:T(8,128)(2,1)}), bf16[192,2240]{1,0:T(8,128)(2,1)}) %reduce-scatter.25.cloned.1.call-update) | async-done | bytes 860176 | tf_op jit(solution)/shard_map/reduce_scatter | solution.py:255
  888.9 2.5 convert_element_type.154
  891.4 129.6 %reduce-scatter.27.cloned.1.call-done = bf16[192,2240]{1,0:T(8,128)(2,1)} async-done(((bf16[1536,2240]{1,0:T(8,128)(2,1)}), bf16[192,2240]{1,0:T(8,128)(2,1)}) %reduce-scatter.27.cloned.1.call-update) | async-done | bytes 860176 | tf_op jit(solution)/shard_map/reduce_scatter | solution.py:258
  1021.0 2.5 convert_element_type.156
  1023.5 129.1 %reduce-scatter.29.cloned.1.call-done = bf16[2240,192]{0,1:T(8,128)(2,1)} async-done(((bf16[2240,1536]{0,1:T(8,128)(2,1)}), bf16[2240,192]{0,1:T(8,128)(2,1)}) %reduce-scatter.29.cloned.1.call-update) | async-done | bytes 860176 | tf_op jit(solution)/shard_map/reduce_scatter | solution.py:261
  1152.6 2.5 convert_element_type.158
  1155.6 63.8 %reduce-scatter.23.cloned.1.call-done = bf16[384,192]{0,1:T(8,128)(2,1)} async-done(((bf16[384,1536]{0,1:T(8,128)(2,1)}), bf16[384,192]{0,1:T(8,128)(2,1)}) %reduce-scatter.23.cloned.1.call-update) | async-done | bytes 147472 | tf_op jit(solution)/shard_map/reduce_scatter | solution.py:252
  1221.0 65.0 %reduce-scatter.19.cloned.1.call-done = bf16[192,384]{1,0:T(8,128)(2,1)} async-done(((bf16[1536,384]{1,0:T(8,128)(2,1)}), bf16[192,384]{1,0:T(8,128)(2,1)}) %reduce-scatter.19.cloned.1.call-update) | async-done | bytes 147472 | tf_op jit(solution)/shard_map/reduce_scatter | solution.py:249
  1287.6 37.9 %reduce-scatter.17.cloned.1.call-done = bf16[256,1536]{1,0:T(8,128)(2,1)} async-done(((bf16[1024,1536]{1,0:T(8,128)(2,1)}), bf16[256,1536]{1,0:T(8,128)(2,1)}) %reduce-scatter.17.cloned.1.call-update) | async-done | bytes 786448 | tf_op jit(solution)/shard_map/reduce_scatter | solution.py:233
  1327.4 39.9 %all-reduce.4 = (f32[1536]{0:T(1024)S(1)}, f32[1536]{0:T(1024)S(1)}, f32[512]{0:T(512)S(1)}, f32[1536]{0:T(1024)S(1)}) all-reduce(f32[1536]{0:T(1024)S(1)} %get-tuple-element.57, f32[1536]{0:T(1024)S(1)} %bitcast_dynamic-update-slice_fusion, ...), channel_id=6, replica_groups=mesh['dp'=8,'tensor'=4] {'dp','tensor'}, use_global_device_ids=true, to_apply=%region_14.15.clone | all-reduce | flops 5120 | bytes 40960
  1369.6 3.8 fusion.13
  1373.4 101.5 %reduce-scatter.21.cloned.1.call-done = f32[48,512]{1,0:T(8,128)} async-done(((f32[1536,512]{1,0:T(8,128)}), f32[48,512]{1,0:T(8,128)}) %reduce-scatter.21.cloned.1.call-update) | async-done | bytes 98320 | tf_op jit(solution)/shard_map/reduce_scatter | solution.py:242
  (159 shorter events, 39.0 us)
Async XLA Ops:
  7.2 5.9 copy-start.25
  7.2 76.3 %copy-start.32 = (f32[384]{0:T(512)S(1)}, f32[384]{0:T(512)}, u32[]{:S(2)}) copy-start(f32[384]{0:T(512)} %param.17) | copy-start | bytes 4612
  7.2 46.8 %all-gather.15.cloned.1.call-start = ((), (), s32[]{:S(2)}) async-start(), calls=%async_computation.12 | async-start | bytes 1327104 | tf_op jit(solution)/shard_map/all_gather | solution.py:62
  7.9 75.5 %all-gather.11.cloned.1.call-start = ((), (), s32[]{:S(2)}) async-start(), calls=%async_computation.10 | async-start | bytes 3932160 | tf_op jit(solution)/shard_map/all_gather | solution.py:130
  9.4 3.7 copy-start.26
  11.7 118.2 %all-gather.13.cloned.1.call-start = ((), (), s32[]{:S(2)}) async-start(), calls=%async_computation.11 | async-start | bytes 1769472 | tf_op jit(solution)/shard_map/all_gather | solution.py:63
  12.4 159.4 %all-gather.17.cloned.1.call-start = ((), (), s32[]{:S(2)}) async-start(), calls=%async_computation.13 | async-start | bytes 1327104 | tf_op jit(solution)/shard_map/all_gather | solution.py:64
  13.0 221.9 %reduce-scatter.11.cloned.1.call-start = ((), (), s32[]{:S(2)}) async-start(), calls=%async_computation.14 | async-start | bytes 7864320 | tf_op jit(solution)/shard_map/reduce_scatter | solution.py:155
  87.1 42.8 %copy-start.33 = (f32[512]{0:T(512)S(1)}, f32[512]{0:T(512)}, u32[]{:S(2)}) copy-start(f32[512]{0:T(512)} %param.19) | copy-start | bytes 6148
  134.1 18.1 %copy-start.22 = (f32[1024,512]{0,1:T(8,128)}, f32[1024,512]{0,1:T(8,128)S(1)}, u32[]{:S(2)}) copy-start(f32[1024,512]{0,1:T(8,128)S(1)} %convolution_add_fusion.1) | copy-start | bytes 6291460
  134.1 4.3 copy-start.7
  138.3 6.5 copy-start.18
  138.9 6.0 copy-start.20
  161.7 15.8 %copy-start.13 = (bf16[1024,3,128]{0,2,1:T(8,128)(2,1)}, bf16[1024,3,128]{0,2,1:T(8,128)(2,1)S(1)}, u32[]{:S(2)}) copy-start(bf16[1024,3,128]{0,2,1:T(8,128)(2,1)S(1)} %get-tuple-element.102) | copy-start | bytes 2359300
  177.5 57.3 %copy-start = (bf16[256,1536]{1,0:T(8,128)(2,1)S(1)}, bf16[256,1536]{1,0:T(8,128)(2,1)}, u32[]{:S(2)}) copy-start(bf16[256,1536]{1,0:T(8,128)(2,1)} %param.13) | copy-start | bytes 2359300
  177.6 59.0 %copy-start.23 = (f32[1536]{0:T(1024)S(1)}, f32[1536]{0:T(1024)}, u32[]{:S(2)}) copy-start(f32[1536]{0:T(1024)} %param.21) | copy-start | bytes 18436
  177.6 168.4 %all-gather.21.cloned.1.call-start = ((), (), s32[]{:S(2)}) async-start(), calls=%async_computation.16 | async-start | bytes 7962624 | tf_op jit(solution)/shard_map/all_gather | solution.py:62
  178.2 196.8 %all-gather.19.cloned.1.call-start = ((), (), s32[]{:S(2)}) async-start(), calls=%async_computation.15 | async-start | bytes 3932160 | tf_op jit(solution)/shard_map/all_gather | solution.py:159
  237.7 248.5 %all-gather.23.cloned.1.call-start = ((), (), s32[]{:S(2)}) async-start(), calls=%async_computation.17 | async-start | bytes 7962624 | tf_op jit(solution)/shard_map/all_gather | solution.py:63
  238.4 276.1 %all-gather.27.cloned.1.call-start = ((), (), s32[]{:S(2)}) async-start(), calls=%async_computation.20 | async-start | bytes 3932160 | tf_op jit(solution)/shard_map/all_gather | solution.py:177
  239.1 386.5 %all-gather.25.cloned.1.call-start = ((), (), s32[]{:S(2)}) async-start(), calls=%async_computation.18 | async-start | bytes 7962624 | tf_op jit(solution)/shard_map/all_gather | solution.py:64
  239.7 484.3 %reduce-scatter.15.cloned.1.call-start = ((), (), s32[]{:S(2)}) async-start(), calls=%async_computation.21 | async-start | bytes 7864320 | tf_op jit(solution)/shard_map/reduce_scatter | solution.py:186
  645.8 11.4 copy-start.28
  645.8 11.4 copy-start.34
  667.4 58.7 %copy-start.3 = (bf16[256,1536]{1,0:T(8,128)(2,1)S(1)}, bf16[256,1536]{1,0:T(8,128)(2,1)}, u32[]{:S(2)}) copy-start(bf16[256,1536]{1,0:T(8,128)(2,1)} %param.25) | copy-start | bytes 2359300
  667.4 97.7 %all-gather.29.cloned.1.call-start = ((), (), s32[]{:S(2)}) async-start(), calls=%async_computation.22 | async-start | bytes 3932160 | tf_op jit(solution)/shard_map/all_gather | solution.py:194
  724.1 2.0 copy-start.2
  727.5 161.4 %reduce-scatter.25.cloned.1.call-start = ((), (), s32[]{:S(2)}) async-start(), calls=%async_computation.27 | async-start | bytes 7962624 | tf_op jit(solution)/shard_map/reduce_scatter | solution.py:255
  739.9 281.1 %reduce-scatter.27.cloned.1.call-start = ((), (), s32[]{:S(2)}) async-start(), calls=%async_computation.28 | async-start | bytes 7962624 | tf_op jit(solution)/shard_map/reduce_scatter | solution.py:258
  752.6 400.0 %reduce-scatter.29.cloned.1.call-start = ((), (), s32[]{:S(2)}) async-start(), calls=%async_computation.29 | async-start | bytes 7962624 | tf_op jit(solution)/shard_map/reduce_scatter | solution.py:261
  765.0 454.3 %reduce-scatter.23.cloned.1.call-start = ((), (), s32[]{:S(2)}) async-start(), calls=%async_computation.26 | async-start | bytes 1327104 | tf_op jit(solution)/shard_map/reduce_scatter | solution.py:252
  765.1 4.3 copy-start.12
  765.1 5.2 copy-start.14
  765.1 5.2 copy-start.30
  773.2 512.8 %reduce-scatter.19.cloned.1.call-start = ((), (), s32[]{:S(2)}) async-start(), calls=%async_computation.24 | async-start | bytes 1327104 | tf_op jit(solution)/shard_map/reduce_scatter | solution.py:249
  773.4 9.4 copy-start.19
  782.8 2.7 copy-start.4
  785.7 2.3 copy-start.29
  790.9 534.7 %reduce-scatter.17.cloned.1.call-start = ((), (), s32[]{:S(2)}) async-start(), calls=%async_computation.23 | async-start | bytes 3932160 | tf_op jit(solution)/shard_map/reduce_scatter | solution.py:233
  801.5 5.3 copy-start.9
  806.7 3.5 copy-start.31
  810.3 1.9 copy-start.6
  810.3 1.9 copy-start.15
  815.8 553.8 %reduce-scatter.13.cloned.1.call-start = ((), (), s32[]{:S(2)}) async-start(), calls=%async_computation.19 | async-start | bytes 3932160 | tf_op jit(solution)/shard_map/reduce_scatter | solution.py:170
  828.6 646.4 %reduce-scatter.21.cloned.1.call-start = ((), (), s32[]{:S(2)}) async-start(), calls=%async_computation.25 | async-start | bytes 3244032 | tf_op jit(solution)/shard_map/reduce_scatter | solution.py:242
  891.4 434.2 %copy-start.1 = (bf16[256,1536]{1,0:T(8,128)(2,1)S(1)}, bf16[256,1536]{1,0:T(8,128)(2,1)}, u32[]{:S(2)}) copy-start(bf16[256,1536]{1,0:T(8,128)(2,1)} %param.13) | copy-start | bytes 2359300
  891.4 434.2 %copy-start.24 = (f32[1536]{0:T(1024)S(1)}, f32[1536]{0:T(1024)}, u32[]{:S(2)}) copy-start(f32[1536]{0:T(1024)} %param.15) | copy-start | bytes 18436
  891.4 434.2 %copy-start.27 = (f32[256]{0:T(256)S(1)}, f32[256]{0:T(256)}, u32[]{:S(2)}) copy-start(f32[256]{0:T(256)} %copy-done.26) | copy-start | bytes 3076
  (7 other events, 6.9 us)
Sparse Core Ops, SparseCore 0:
  10.2 43.7 all-gather.14
  56.1 27.2 all-gather.10
  85.7 44.1 all-gather.12
  131.9 39.8 all-gather.16
  177.7 57.1 reduce-scatter.10
  237.1 108.7 all-gather.20
  348.2 26.7 all-gather.18
  377.3 108.7 all-gather.22
  487.8 26.7 all-gather.26
  516.8 108.7 all-gather.24
  667.5 56.5 reduce-scatter.14
  727.6 28.5 all-gather.28
  759.9 129.0 reduce-scatter.24
  892.9 128.0 reduce-scatter.26
  1024.5 128.0 reduce-scatter.28
  1156.2 63.0 reduce-scatter.22
  1222.9 62.9 reduce-scatter.18
  1288.5 36.9 reduce-scatter.16
  1328.1 38.3 reduce-scatter.12
  1373.2 101.6 reduce-scatter.20
where the time goes:
time: 1490 us; the launch traced here: 1480 us
  waiting for transfers between devices  1180 us (79%)
  matrix products  193 us (13%)
  other arithmetic  42.9 us (3%)
  blocking collectives  39.9 us (3%)
  between operations  15.1 us (1%)
    dot_general x18, matrix products, matmul(): return jnp.dot(left, right, preferred_element_type=jnp.float32)  152 us
    all_gather x2, waiting for transfers between devices, gather_three(): lax.all_gather(first, 'dp', axis=0, tiled=True)  146 us
    all_gather x2, waiting for transfers between devices, gather_three(): lax.all_gather(second, 'dp', axis=0, tiled=True)  140 us
    reduce_scatter x1, waiting for transfers between devices, local(): lax.psum_scatter(grad_up_w.astype(jnp.bfloat16), 'dp', scatter_dimension=...  130 us
    reduce_scatter x1, waiting for transfers between devices, local(): lax.psum_scatter(grad_down_w.astype(jnp.bfloat16), 'dp', scatter_dimensio...  129 us
    all_gather x2, waiting for transfers between devices, gather_three(): lax.all_gather(third, 'dp', axis=1, tiled=True)  121 us
    reduce_scatter x1, waiting for transfers between devices, local(): lax.psum_scatter(grad_keyval_w, ('dp', 'tensor'), scatter_dimension=0, ti...  101 us
    reduce_scatter x1, waiting for transfers between devices, local(): lax.psum_scatter(grad_query_w.astype(jnp.bfloat16), 'dp', scatter_dimensi...  65 us
  transfers between devices with their start and end apart: 20, of which 18 were waited for; matrix products, arithmetic and copies ran while one was open for 13% of the time, Pallas kernels for 0%

commit v1 on v0

--- a/solution.py
+++ b/solution.py
@@ -1,8 +1,10 @@
+import functools
 import math
 import jax
 import jax.numpy as jnp
 from jax import lax
 from jax.sharding import PartitionSpec as P
+from jax.lax import axis_index, axis_size, ppermute
 
 HQ = 12
 KV = 2
@@ -12,6 +14,34 @@
 masked_score = -1e30
 
 
+def _resolve_panel(own_rows, dim_k):
+    fresh = list(own_rows.shape[1:])
+    fresh[dim_k] *= own_rows.shape[0]
+    return jnp.moveaxis(own_rows, 0, dim_k).reshape(fresh)
+
+
+def _check_numbers(a0, comm_axis, array_dim):
+    world_n = axis_size(comm_axis)
+    seen = [(dev, (dev + 1) % world_n) for dev in range(world_n)]
+    buffer = [(hop_no, p) for p, hop_no in seen]
+    block_next, response = ([], [])
+    for j in range(world_n - 1):
+        if j % 2 == 0:
+            n_now = ppermute(block_next[-1] if block_next else a0, comm_axis, seen)
+            block_next.append(n_now)
+        else:
+            response.append(ppermute(response[-1] if response else a0, comm_axis, buffer))
+    long_array = jnp.stack([*block_next[::-1], a0, *response], axis=0)
+    f_next = axis_index(comm_axis)
+    r2 = len(block_next)
+    item_now = f_next - r2
+    long_array = long_array[(jnp.arange(world_n) - item_now) % world_n]
+    return _resolve_panel(long_array, array_dim)
+
+
+lift_islands = functools.partial(_check_numbers, comm_axis="dp", array_dim=1)
+
+
 def matmul(left, right):
     return jnp.dot(left, right, preferred_element_type=jnp.float32)
 
@@ -61,7 +91,7 @@
     return (
         lax.all_gather(first, "dp", axis=0, tiled=True),
         lax.all_gather(second, "dp", axis=0, tiled=True),
-        lax.all_gather(third, "dp", axis=1, tiled=True),
+        lift_islands(third),
     )
 
 

time: 1490 us -> 1480 us (level)
  waiting for transfers between devices: 1180 us -> 1060 us
  starting transfers between devices: 1.6 us -> 90.7 us
  local copies, waits for them, and re-layouts: 11.4 us -> 34 us
    all_gather x2, waiting for transfers between devices: 146 us -> 6.18 us  [gather_three(): lax.all_gather(first, 'dp', axis=0, tiled=True)]
    ppermute x0 -> x14, waiting for transfers between devices: none -> 136 us  [the longest x8 121 us: _check_numbers(): n_now = ppermute(block_next[-1] if block_next else a0, comm_axis, seen)]
    all_gather x2 -> x0, waiting for transfers between devices: 121 us -> none  [gather_three(): lax.all_gather(third, 'dp', axis=1, tiled=True)]
    ppermute x0 -> x14, starting transfers between devices: none -> 89.1 us  [the longest x6 77.8 us: _check_numbers(): ppermute(response[-1] if response else a0, comm_axis, buffer)]
  transfers between devices with their start and end apart: 20 -> 32, of which waited for: 18 -> 26; matrix products, arithmetic and copies ran while one was open for 13% -> 12% of each run, Pallas kernels for 0% -> 0%
where the time goes in v1:
time: 1480 us; the launch traced here: 1470 us
  waiting for transfers between devices  1060 us (72%)
  matrix products  193 us (13%)
  starting transfers between devices  90.7 us (6%)
  other arithmetic  43.8 us (3%)
  blocking collectives  39.9 us (3%)
  local copies, waits for them, and re-layouts  34 us (2%)
  between operations  15.3 us (1%)
    dot_general x18, matrix products, matmul(): return jnp.dot(left, right, preferred_element_type=jnp.float32)  153 us
    all_gather x2, waiting for transfers between devices, gather_three(): lax.all_gather(second, 'dp', axis=0, tiled=True)  140 us
    reduce_scatter x1, waiting for transfers between devices, local(): lax.psum_scatter(grad_up_w.astype(jnp.bfloat16), 'dp', scatter_dimension=...  130 us
    reduce_scatter x1, waiting for transfers between devices, local(): lax.psum_scatter(grad_down_w.astype(jnp.bfloat16), 'dp', scatter_dimensio...  129 us
    ppermute x8, waiting for transfers between devices, _check_numbers(): n_now = ppermute(block_next[-1] if block_next else a0, comm_axis, seen)  121 us
    reduce_scatter x1, waiting for transfers between devices, local(): lax.psum_scatter(grad_keyval_w, ('dp', 'tensor'), scatter_dimension=0, ti...  101 us
    ppermute x6, starting transfers between devices, _check_numbers(): ppermute(response[-1] if response else a0, comm_axis, buffer)  77.8 us
    reduce_scatter x1, waiting for transfers between devices, local(): lax.psum_scatter(grad_query_w.astype(jnp.bfloat16), 'dp', scatter_dimensi...  65.1 us
  transfers between devices with their start and end apart: 32, of which 26 were waited for; matrix products, arithmetic and copies ran while one was open for 12% of the time, Pallas kernels for 0%

profile of v1, /device:TPU:0, one launch (start us, length us, event | category | flops | bytes accessed | tf_op | source)
XLA Modules:
  0.0 1474.4 jit_solution(7158856816049792713)
XLA Ops:
  23.5 9.5 collective-permute-done.1
  33.1 4.8 collective-permute-start.5
  42.8 5.2 collective-permute-start.6
  53.7 6.2 all-gather.13.cloned.1.call-done
  59.9 29.5 %all-gather.9.cloned.1.call-done = bf16[1024,1536]{1,0:T(8,128)(2,1)} async-done(((bf16[256,1536]{1,0:T(8,128)(2,1)}), bf16[1024,1536]{1,0:T(8,128)(2,1)}) %all-gather.9.cloned.1.call-update) | async-done | bytes 3145744 | tf_op jit(solution)/shard_map/all_gather | solution.py:160
  94.3 41.5 %all-gather.11.cloned.1.call-done = bf16[1536,512]{1,0:T(8,128)(2,1)} async-done(((bf16[192,512]{1,0:T(8,128)(2,1)}), bf16[1536,512]{1,0:T(8,128)(2,1)}) %all-gather.11.cloned.1.call-update) | async-done | bytes 1572880 | tf_op jit(solution)/shard_map/all_gather | solution.py:93
  135.8 4.2 convolution_add_fusion.1
  144.6 5.9 fusion.8
  150.6 7.3 exponential_reduce_fusion
  157.9 9.3 bitcast_convert_fusion
  168.2 4.5 fusion.52
  173.3 56.7 %reduce-scatter.11.cloned.1.call-done = f32[256,1536]{1,0:T(8,128)} async-done(((f32[1024,1536]{1,0:T(8,128)}), f32[256,1536]{1,0:T(8,128)}) %reduce-scatter.11.cloned.1.call-update) | async-done | bytes 1572880 | tf_op jit(solution)/shard_map/reduce_scatter | solution.py:185
  235.1 35.0 %collective-permute-done.7 = bf16[2240,192]{0,1:T(8,128)(2,1)S(1)} collective-permute-done((bf16[2240,192]{0,1:T(8,128)(2,1)S(1)}, bf16[2240,192]{0,1:T(8,128)(2,1)S(1)}, u32[]{:S(2)}, u32[]{:S(2)}) %collective-permute-start.7) | collective-permute-done | bytes 860192 | tf_op jit(solution)/shard_map/ppermute | solution.py:30
  270.1 4.7 collective-permute-start.11
  274.9 38.7 %collective-permute-done.8 = bf16[2240,192]{0,1:T(8,128)(2,1)S(1)} collective-permute-done((bf16[2240,192]{0,1:T(8,128)(2,1)S(1)}, bf16[2240,192]{0,1:T(8,128)(2,1)S(1)}, u32[]{:S(2)}, u32[]{:S(2)}) %collective-permute-start.8) | collective-permute-done | bytes 860192 | tf_op jit(solution)/shard_map/ppermute | solution.py:30
  316.1 35.8 %collective-permute-start.12 = (bf16[2240,192]{0,1:T(8,128)(2,1)}, bf16[2240,192]{0,1:T(8,128)(2,1)}, u32[]{:S(2)}, u32[]{:S(2)}) collective-permute-start(bf16[2240,192]{0,1:T(8,128)(2,1)} %collective-permute-done.11), channel_id=1, source_target_pairs={{4,0},{8,4},{12,8},{16,12},{20,16},{24,20},{28,24},{0,28},{5,1},{9... | collective-permute-start | bytes 2580488 | tf_op jit(solution)/shard_map/ppermute | solution.py:33
  351.9 20.8 %collective-permute-done.9 = bf16[2240,192]{0,1:T(8,128)(2,1)} collective-permute-done((bf16[2240,192]{0,1:T(8,128)(2,1)S(1)}, bf16[2240,192]{0,1:T(8,128)(2,1)}, u32[]{:S(2)}, u32[]{:S(2)}) %collective-permute-start.9) | collective-permute-done | bytes 860192 | tf_op jit(solution)/shard_map/ppermute | solution.py:30
  375.4 11.4 collective-permute-done.12
  386.8 24.1 %collective-permute-start.13 = (bf16[2240,192]{0,1:T(8,128)(2,1)}, bf16[2240,192]{0,1:T(8,128)(2,1)S(1)}, u32[]{:S(2)}, u32[]{:S(2)}) collective-permute-start(bf16[2240,192]{0,1:T(8,128)(2,1)} %collective-permute-done.12), channel_id=1, source_target_pairs={{4,0},{8,4},{12,8},{16,12},{20,16},{24,20},{28,24},{0,28},{5,1},{9... | collective-permute-start | bytes 2580488 | tf_op jit(solution)/shard_map/ppermute | solution.py:33
  410.9 9.6 collective-permute-done.10
  433.1 6.8 gather_fusion.1
  439.9 34.2 %all-gather.15.cloned.1.call-done = bf16[1024,1536]{1,0:T(8,128)(2,1)} async-done(((bf16[256,1536]{1,0:T(8,128)(2,1)}), bf16[1024,1536]{1,0:T(8,128)(2,1)}) %all-gather.15.cloned.1.call-update) | async-done | bytes 3145744 | tf_op jit(solution)/shard_map/all_gather | solution.py:189
  474.1 13.2 fusion.53
  487.3 98.1 %all-gather.19.cloned.1.call-done = bf16[1536,2240]{1,0:T(8,128)(2,1)} async-done(((bf16[192,2240]{1,0:T(8,128)(2,1)}), bf16[1536,2240]{1,0:T(8,128)(2,1)}) %all-gather.19.cloned.1.call-update) | async-done | bytes 6881296 | tf_op jit(solution)/shard_map/all_gather | solution.py:93
  585.3 13.2 fusion.54
  598.5 15.2 %all-gather.21.cloned.1.call-done = bf16[1024,1536]{1,0:T(8,128)(2,1)} async-done(((bf16[256,1536]{1,0:T(8,128)(2,1)}), bf16[1024,1536]{1,0:T(8,128)(2,1)}) %all-gather.21.cloned.1.call-update) | async-done | bytes 3145744 | tf_op jit(solution)/shard_map/all_gather | solution.py:207
  613.7 22.9 %fusion.6 = (bf16[1024,2240]{0,1:T(8,128)(2,1)}, bf16[1024,2240]{0,1:T(8,128)(2,1)}, bf16[1024,2240]{0,1:T(8,128)(2,1)}) fusion(f32[1024,2240]{0,1:T(8,128)} %fusion.53, f32[1024,2240]{0,1:T(8,128)} %fusion.54, bf16[2240,1536]{0,1:T(8,128)(2,1)} %bitcast.167, bf16[1024,1536]{1,0:T(8,128)(2,1)} %all-gather.21.cloned.1.call-done), kind=kOutput, calls=%fused_computation.17 | convolution fusion | flops 7080837120 | bytes 42139648 | tf_op jit(solution)/shard_map/dot_general | solution.py:46
  636.6 11.4 fusion.55
  648.0 9.8 convolution_add_fusion
  657.9 58.4 %reduce-scatter.15.cloned.1.call-done = f32[256,1536]{1,0:T(8,128)} async-done(((f32[1024,1536]{1,0:T(8,128)}), f32[256,1536]{1,0:T(8,128)}) %reduce-scatter.15.cloned.1.call-update) | async-done | bytes 1572880 | tf_op jit(solution)/shard_map/reduce_scatter | solution.py:216
  719.9 12.3 convolution_convert_fusion.2
  732.3 12.7 convolution_convert_fusion.1
  745.0 12.4 convolution_convert_fusion
  758.6 3.9 convolution_convert_fusion.6
  766.8 9.3 fusion.1
  784.4 9.0 fusion.51
  794.5 5.2 fusion.26
  809.1 12.5 convolution_convert_fusion.3
  822.8 5.4 fusion.57
  828.2 53.0 %reduce-scatter.25.cloned.1.call-done = bf16[192,2240]{1,0:T(8,128)(2,1)} async-done(((bf16[1536,2240]{1,0:T(8,128)(2,1)}), bf16[192,2240]{1,0:T(8,128)(2,1)}) %reduce-scatter.25.cloned.1.call-update) | async-done | bytes 860176 | tf_op jit(solution)/shard_map/reduce_scatter | solution.py:285
  883.7 129.6 %reduce-scatter.27.cloned.1.call-done = bf16[192,2240]{1,0:T(8,128)(2,1)} async-done(((bf16[1536,2240]{1,0:T(8,128)(2,1)}), bf16[192,2240]{1,0:T(8,128)(2,1)}) %reduce-scatter.27.cloned.1.call-update) | async-done | bytes 860176 | tf_op jit(solution)/shard_map/reduce_scatter | solution.py:288
  1015.8 129.3 %reduce-scatter.29.cloned.1.call-done = bf16[2240,192]{0,1:T(8,128)(2,1)} async-done(((bf16[2240,1536]{0,1:T(8,128)(2,1)}), bf16[2240,192]{0,1:T(8,128)(2,1)}) %reduce-scatter.29.cloned.1.call-update) | async-done | bytes 860176 | tf_op jit(solution)/shard_map/reduce_scatter | solution.py:291
  1148.0 63.8 %reduce-scatter.23.cloned.1.call-done = bf16[384,192]{0,1:T(8,128)(2,1)} async-done(((bf16[384,1536]{0,1:T(8,128)(2,1)}), bf16[384,192]{0,1:T(8,128)(2,1)}) %reduce-scatter.23.cloned.1.call-update) | async-done | bytes 147472 | tf_op jit(solution)/shard_map/reduce_scatter | solution.py:282
  1213.5 65.1 %reduce-scatter.19.cloned.1.call-done = bf16[192,384]{1,0:T(8,128)(2,1)} async-done(((bf16[1536,384]{1,0:T(8,128)(2,1)}), bf16[192,384]{1,0:T(8,128)(2,1)}) %reduce-scatter.19.cloned.1.call-update) | async-done | bytes 147472 | tf_op jit(solution)/shard_map/reduce_scatter | solution.py:279
  1280.2 37.9 %reduce-scatter.17.cloned.1.call-done = bf16[256,1536]{1,0:T(8,128)(2,1)} async-done(((bf16[1024,1536]{1,0:T(8,128)(2,1)}), bf16[256,1536]{1,0:T(8,128)(2,1)}) %reduce-scatter.17.cloned.1.call-update) | async-done | bytes 786448 | tf_op jit(solution)/shard_map/reduce_scatter | solution.py:263
  1319.9 39.9 %all-reduce.4 = (f32[1536]{0:T(1024)S(1)}, f32[1536]{0:T(1024)S(1)}, f32[512]{0:T(512)S(1)}, f32[1536]{0:T(1024)S(1)}) all-reduce(f32[1536]{0:T(1024)S(1)} %get-tuple-element.57, f32[1536]{0:T(1024)S(1)} %bitcast_dynamic-update-slice_fusion.16, ...), channel_id=6, replica_groups=mesh['dp'=8,'tensor'=4] {'dp','tensor'}, use_global_device_ids=true, to_apply=%region_14.15.clone | all-reduce | flops 5120 | bytes 40960
  1362.2 3.8 fusion.17
  1366.0 101.3 %reduce-scatter.21.cloned.1.call-done = f32[48,512]{1,0:T(8,128)} async-done(((f32[1536,512]{1,0:T(8,128)}), f32[48,512]{1,0:T(8,128)}) %reduce-scatter.21.cloned.1.call-update) | async-done | bytes 98320 | tf_op jit(solution)/shard_map/reduce_scatter | solution.py:272
  (235 shorter events, 104.9 us)
Async XLA Ops:
  7.2 52.7 %all-gather.13.cloned.1.call-start = ((), (), s32[]{:S(2)}) async-start(), calls=%async_computation.12 | async-start | bytes 1327104 | tf_op jit(solution)/shard_map/all_gather | solution.py:92
  7.9 81.5 %all-gather.9.cloned.1.call-start = ((), (), s32[]{:S(2)}) async-start(), calls=%async_computation.10 | async-start | bytes 3932160 | tf_op jit(solution)/shard_map/all_gather | solution.py:160
  11.7 124.2 %all-gather.11.cloned.1.call-start = ((), (), s32[]{:S(2)}) async-start(), calls=%async_computation.11 | async-start | bytes 1769472 | tf_op jit(solution)/shard_map/all_gather | solution.py:93
  11.7 10.0 collective-permute-start
  14.7 18.3 %collective-permute-start.4 = (bf16[384,192]{0,1:T(8,128)(2,1)S(1)}, bf16[384,192]{0,1:T(8,128)(2,1)S(1)}, u32[]{:S(2)}, u32[]{:S(2)}) collective-permute-start(bf16[384,192]{0,1:T(8,128)(2,1)S(1)} %copy-done.33), channel_id=1, source_target_pairs={{4,0},{8,4},{12,8},{16,12},{20,16},{24,20},{28,24},{0,28},{5,1},{9... | collective-permute-start | bytes 442376 | tf_op jit(solution)/shard_map/ppermute | solution.py:33
  17.9 212.1 %reduce-scatter.11.cloned.1.call-start = ((), (), s32[]{:S(2)}) async-start(), calls=%async_computation.13 | async-start | bytes 7864320 | tf_op jit(solution)/shard_map/reduce_scatter | solution.py:185
  18.0 71.4 %copy-start.49 = (f32[384]{0:T(512)S(1)}, f32[384]{0:T(512)}, u32[]{:S(2)}) copy-start(f32[384]{0:T(512)} %param.17) | copy-start | bytes 4612
  21.7 11.2 collective-permute-start.1
  32.9 7.9 collective-permute-start.2
  33.1 9.7 collective-permute-start.5
  40.9 10.4 collective-permute-start.3
  42.8 10.1 collective-permute-start.6
  53.7 113.6 %copy-start.4 = (bf16[8,384,192]{1,2,0:T(8,128)(2,1)}, bf16[8,384,192]{1,2,0:T(8,128)(2,1)S(1)}, u32[]{:S(2)}) copy-start(bf16[8,384,192]{1,2,0:T(8,128)(2,1)S(1)} %gather_fusion) | copy-start | bytes 3538948
  93.0 42.8 %copy-start.50 = (f32[512]{0:T(512)S(1)}, f32[512]{0:T(512)}, u32[]{:S(2)}) copy-start(f32[512]{0:T(512)} %param.19) | copy-start | bytes 6148
  172.6 57.4 %copy-start = (bf16[256,1536]{1,0:T(8,128)(2,1)S(1)}, bf16[256,1536]{1,0:T(8,128)(2,1)}, u32[]{:S(2)}) copy-start(bf16[256,1536]{1,0:T(8,128)(2,1)} %param.13) | copy-start | bytes 2359300
  172.6 59.1 %copy-start.34 = (f32[1536]{0:T(1024)S(1)}, f32[1536]{0:T(1024)}, u32[]{:S(2)}) copy-start(f32[1536]{0:T(1024)} %param.21) | copy-start | bytes 18436
  172.7 267.2 %all-gather.17.cloned.1.call-start = ((), (), s32[]{:S(2)}) async-start(), calls=%async_computation.15 | async-start | bytes 7962624 | tf_op jit(solution)/shard_map/all_gather | solution.py:92
  173.3 60.4 %copy-start.25 = (bf16[2240,192]{0,1:T(8,128)(2,1)S(1)}, bf16[2240,192]{0,1:T(8,128)(2,1)}, u32[]{:S(2)}) copy-start(bf16[2240,192]{0,1:T(8,128)(2,1)} %param.24) | copy-start | bytes 2580484
  173.3 300.8 %all-gather.15.cloned.1.call-start = ((), (), s32[]{:S(2)}) async-start(), calls=%async_computation.14 | async-start | bytes 3932160 | tf_op jit(solution)/shard_map/all_gather | solution.py:189
  231.7 486.7 %copy-start.37 = (f32[256]{0:T(256)}, f32[256]{0:T(256)S(1)}, u32[]{:S(2)}) copy-start(f32[256]{0:T(256)S(1)} %add_rsqrt_fusion) | copy-start | bytes 3076
  232.8 352.5 %all-gather.19.cloned.1.call-start = ((), (), s32[]{:S(2)}) async-start(), calls=%async_computation.16 | async-start | bytes 7962624 | tf_op jit(solution)/shard_map/all_gather | solution.py:93
  233.6 380.1 %all-gather.21.cloned.1.call-start = ((), (), s32[]{:S(2)}) async-start(), calls=%async_computation.18 | async-start | bytes 3932160 | tf_op jit(solution)/shard_map/all_gather | solution.py:207
  233.6 36.5 %collective-permute-start.7 = (bf16[2240,192]{0,1:T(8,128)(2,1)S(1)}, bf16[2240,192]{0,1:T(8,128)(2,1)S(1)}, u32[]{:S(2)}, u32[]{:S(2)}) collective-permute-start(bf16[2240,192]{0,1:T(8,128)(2,1)S(1)} %copy-done.25), channel_id=1, source_target_pairs={{0,4},{4,8},{8,12},{12,16},{16,20},{20,24},{24,28},{28,0},{1,5},{5... | collective-permute-start | bytes 2580488 | tf_op jit(solution)/shard_map/ppermute | solution.py:30
  270.1 45.9 %copy-start.26 = (bf16[2240,192]{0,1:T(8,128)(2,1)}, bf16[2240,192]{0,1:T(8,128)(2,1)S(1)}, u32[]{:S(2)}) copy-start(bf16[2240,192]{0,1:T(8,128)(2,1)S(1)} %collective-permute-done.7) | copy-start | bytes 2580484
  270.1 43.5 %collective-permute-start.8 = (bf16[2240,192]{0,1:T(8,128)(2,1)S(1)}, bf16[2240,192]{0,1:T(8,128)(2,1)S(1)}, u32[]{:S(2)}, u32[]{:S(2)}) collective-permute-start(bf16[2240,192]{0,1:T(8,128)(2,1)S(1)} %collective-permute-done.7), channel_id=1, source_target_pairs={{0,4},{4,8},{8,12},{12,16},{16,20},{20,24},{24,28},{28,0},{1,5},{5... | collective-permute-start | bytes 2580488 | tf_op jit(solution)/shard_map/ppermute | solution.py:30
  270.1 45.9 %collective-permute-start.11 = (bf16[2240,192]{0,1:T(8,128)(2,1)S(1)}, bf16[2240,192]{0,1:T(8,128)(2,1)}, u32[]{:S(2)}, u32[]{:S(2)}) collective-permute-start(bf16[2240,192]{0,1:T(8,128)(2,1)S(1)} %copy-done.25), channel_id=1, source_target_pairs={{4,0},{8,4},{12,8},{16,12},{20,16},{24,20},{28,24},{0,28},{5,1},{9... | collective-permute-start | bytes 2580488 | tf_op jit(solution)/shard_map/ppermute | solution.py:33
  313.6 59.1 %collective-permute-start.9 = (bf16[2240,192]{0,1:T(8,128)(2,1)S(1)}, bf16[2240,192]{0,1:T(8,128)(2,1)}, u32[]{:S(2)}, u32[]{:S(2)}) collective-permute-start(bf16[2240,192]{0,1:T(8,128)(2,1)S(1)} %collective-permute-done.8), channel_id=1, source_target_pairs={{0,4},{4,8},{8,12},{12,16},{16,20},{20,24},{24,28},{28,0},{1,5},{5... | collective-permute-start | bytes 2580488 | tf_op jit(solution)/shard_map/ppermute | solution.py:30
  316.1 70.7 %collective-permute-start.12 = (bf16[2240,192]{0,1:T(8,128)(2,1)}, bf16[2240,192]{0,1:T(8,128)(2,1)}, u32[]{:S(2)}, u32[]{:S(2)}) collective-permute-start(bf16[2240,192]{0,1:T(8,128)(2,1)} %collective-permute-done.11), channel_id=1, source_target_pairs={{4,0},{8,4},{12,8},{16,12},{20,16},{24,20},{28,24},{0,28},{5,1},{9... | collective-permute-start | bytes 2580488 | tf_op jit(solution)/shard_map/ppermute | solution.py:33
  372.7 47.7 %collective-permute-start.10 = (bf16[2240,192]{0,1:T(8,128)(2,1)}, bf16[2240,192]{0,1:T(8,128)(2,1)}, u32[]{:S(2)}, u32[]{:S(2)}) collective-permute-start(bf16[2240,192]{0,1:T(8,128)(2,1)} %collective-permute-done.9), channel_id=1, source_target_pairs={{0,4},{4,8},{8,12},{12,16},{16,20},{20,24},{24,28},{28,0},{1,5},{5... | collective-permute-start | bytes 2580488 | tf_op jit(solution)/shard_map/ppermute | solution.py:30
  375.3 341.1 %reduce-scatter.15.cloned.1.call-start = ((), (), s32[]{:S(2)}) async-start(), calls=%async_computation.19 | async-start | bytes 7864320 | tf_op jit(solution)/shard_map/reduce_scatter | solution.py:216
  375.3 49.4 %copy-start.29 = (bf16[2240,192]{0,1:T(8,128)(2,1)S(1)}, bf16[2240,192]{0,1:T(8,128)(2,1)}, u32[]{:S(2)}) copy-start(bf16[2240,192]{0,1:T(8,128)(2,1)} %copy-done.28) | copy-start | bytes 2580484
  375.4 50.4 %copy-start.27 = (bf16[2240,192]{0,1:T(8,128)(2,1)S(1)}, bf16[2240,192]{0,1:T(8,128)(2,1)}, u32[]{:S(2)}) copy-start(bf16[2240,192]{0,1:T(8,128)(2,1)} %copy-done.26) | copy-start | bytes 2580484
  386.8 45.3 %collective-permute-start.13 = (bf16[2240,192]{0,1:T(8,128)(2,1)}, bf16[2240,192]{0,1:T(8,128)(2,1)S(1)}, u32[]{:S(2)}, u32[]{:S(2)}) collective-permute-start(bf16[2240,192]{0,1:T(8,128)(2,1)} %collective-permute-done.12), channel_id=1, source_target_pairs={{4,0},{8,4},{12,8},{16,12},{20,16},{24,20},{28,24},{0,28},{5,1},{9... | collective-permute-start | bytes 2580488 | tf_op jit(solution)/shard_map/ppermute | solution.py:33
  657.9 60.5 %copy-start.3 = (bf16[256,1536]{1,0:T(8,128)(2,1)S(1)}, bf16[256,1536]{1,0:T(8,128)(2,1)}, u32[]{:S(2)}) copy-start(bf16[256,1536]{1,0:T(8,128)(2,1)} %param.25) | copy-start | bytes 2359300
  657.9 99.5 %all-gather.23.cloned.1.call-start = ((), (), s32[]{:S(2)}) async-start(), calls=%async_computation.20 | async-start | bytes 3932160 | tf_op jit(solution)/shard_map/all_gather | solution.py:224
  719.8 161.4 %reduce-scatter.25.cloned.1.call-start = ((), (), s32[]{:S(2)}) async-start(), calls=%async_computation.25 | async-start | bytes 7962624 | tf_op jit(solution)/shard_map/reduce_scatter | solution.py:285
  732.2 281.1 %reduce-scatter.27.cloned.1.call-start = ((), (), s32[]{:S(2)}) async-start(), calls=%async_computation.26 | async-start | bytes 7962624 | tf_op jit(solution)/shard_map/reduce_scatter | solution.py:288
  744.9 400.1 %reduce-scatter.29.cloned.1.call-start = ((), (), s32[]{:S(2)}) async-start(), calls=%async_computation.27 | async-start | bytes 7962624 | tf_op jit(solution)/shard_map/reduce_scatter | solution.py:291
  757.4 454.5 %reduce-scatter.23.cloned.1.call-start = ((), (), s32[]{:S(2)}) async-start(), calls=%async_computation.24 | async-start | bytes 1327104 | tf_op jit(solution)/shard_map/reduce_scatter | solution.py:282
  766.3 512.2 %reduce-scatter.19.cloned.1.call-start = ((), (), s32[]{:S(2)}) async-start(), calls=%async_computation.22 | async-start | bytes 1327104 | tf_op jit(solution)/shard_map/reduce_scatter | solution.py:279
  784.2 533.9 %reduce-scatter.17.cloned.1.call-start = ((), (), s32[]{:S(2)}) async-start(), calls=%async_computation.21 | async-start | bytes 3932160 | tf_op jit(solution)/shard_map/reduce_scatter | solution.py:263
  808.8 553.3 %reduce-scatter.13.cloned.1.call-start = ((), (), s32[]{:S(2)}) async-start(), calls=%async_computation.17 | async-start | bytes 3932160 | tf_op jit(solution)/shard_map/reduce_scatter | solution.py:200
  821.6 645.7 %reduce-scatter.21.cloned.1.call-start = ((), (), s32[]{:S(2)}) async-start(), calls=%async_computation.23 | async-start | bytes 3244032 | tf_op jit(solution)/shard_map/reduce_scatter | solution.py:272
  883.7 434.4 %copy-start.1 = (bf16[256,1536]{1,0:T(8,128)(2,1)S(1)}, bf16[256,1536]{1,0:T(8,128)(2,1)}, u32[]{:S(2)}) copy-start(bf16[256,1536]{1,0:T(8,128)(2,1)} %param.13) | copy-start | bytes 2359300
  883.7 434.4 %copy-start.35 = (f32[1536]{0:T(1024)S(1)}, f32[1536]{0:T(1024)}, u32[]{:S(2)}) copy-start(f32[1536]{0:T(1024)} %param.15) | copy-start | bytes 18436
  883.7 434.4 %copy-start.42 = (f32[256]{0:T(256)S(1)}, f32[256]{0:T(256)}, u32[]{:S(2)}) copy-start(f32[256]{0:T(256)} %copy-done.41) | copy-start | bytes 3076
  1015.8 346.3 %copy-start.38 = (f32[256]{0:T(256)S(1)}, f32[256]{0:T(256)}, u32[]{:S(2)}) copy-start(f32[256]{0:T(256)} %copy-done.37) | copy-start | bytes 3076
  1015.8 346.3 %copy-start.44 = (f32[256]{0:T(256)S(1)}, f32[256]{0:T(256)}, u32[]{:S(2)}) copy-start(f32[256]{0:T(256)} %copy-done.43) | copy-start | bytes 3076
  (36 other events, 202.9 us)
Sparse Core Ops, SparseCore 0:
  10.2 49.6 all-gather.12
  62.0 27.3 all-gather.8
  91.6 44.1 all-gather.10
  172.8 57.1 reduce-scatter.10
  232.3 204.5 all-gather.16
  438.9 35.1 all-gather.14
  476.5 108.7 all-gather.18
  587.0 26.7 all-gather.20
  658.0 58.3 reduce-scatter.14
  719.9 28.5 all-gather.22
  752.2 128.9 reduce-scatter.24
  885.2 128.0 reduce-scatter.26
  1017.0 128.0 reduce-scatter.28
  1148.7 63.1 reduce-scatter.22
  1215.5 63.0 reduce-scatter.18
  1281.1 36.9 reduce-scatter.16
  1320.5 38.2 reduce-scatter.12
  1365.6 101.7 reduce-scatter.20
